TPU v7x, 256 devices: a whole 4x4x8 slice. The times are simulated.
256 devices in a mesh: row: 16 (over y_hi, x, core), col: 16 (over y_lo, z).
Axes of the slice: x: 4, y: 4 (y_hi: 2, y_lo: 2; y = y_hi * 2 + y_lo), z: 8, core: 2. Of those that a mesh axis runs over, the one named last changes fastest.
Arguments:
- op_tiles: float32 [512, 16, 64, 64], P('row', 'col'), may hold values from -18 to 18
- op_rows: int32 [512, 16], P('row', 'col'), may hold values from 0 to 7
- op_cols: int32 [512, 16], P('row', 'col'), may hold values from 0 to 7
- op_count: int32 [16, 16], P('row', 'col'), may hold values from 1 to 32, as said below
- pro_tiles: float32 [128, 16, 64, 64], P('row', 'col'), may hold values from -0.125 to 0.125
- pro_cols: int32 [128, 16], P('row', 'col'), may hold values from 0 to 1
- pro_live: int32 [128, 16], P('row', 'col'), may hold values 0 or 1
Outputs:
- product: float32 [128, 32, 64, 64], P('row', 'col')
- coarse: float32 [32, 32, 64, 64], P('row', 'col')
Inputs may be any that keep to these rules, and one draw needn't show every extreme that they name: `op_count`: live slots of each device's list; some device's list is full in every draw.
All inputs are finite; a program needn't handle non-finite values. No bound on the sum of `pro_live` on one device may be relied on, other than what follows from the above.
Results may differ from a plain program's by a relative error of at most 0.0003.
Values sent between devices are 32-bit elements; how exact they have to be, the bound alone decides.
A program may use at most 128 MiB of HBM per device.

v0:
```python
import jax
import jax.numpy as jnp
from jax import lax
from jax.sharding import PartitionSpec as P

COARSEN = 4
precise = lax.Precision.HIGHEST


def broadcast(value, axis, root):
    mine = lax.axis_index(axis) == root
    return lax.psum(jnp.where(mine, value, jnp.zeros_like(value)), axis)


def column_panel(masked_pro, pro_cols):
    return (
        lax.all_gather(masked_pro, "row", axis=0, tiled=True),
        lax.all_gather(pro_cols, "row", axis=0, tiled=True),
    )


def shards(op_tiles, op_rows, op_cols, op_count, pro_tiles, pro_cols, pro_live):
    list_len = op_tiles.shape[0]
    tile_size = op_tiles.shape[2]
    fine_rows = pro_tiles.shape[0]
    row_count = lax.axis_size("row")
    col_count = lax.axis_size("col")
    fine_total = fine_rows * row_count
    fine_cols = fine_total // col_count
    coarse_total = fine_total // COARSEN
    coarse_cols = coarse_total // col_count
    coarse_rows = coarse_total // row_count
    row_index = lax.axis_index("row")
    col_index = lax.axis_index("col")
    live_op = (jnp.arange(list_len, dtype=jnp.int32) < op_count[0, 0]).astype(jnp.float32)
    masked_op = op_tiles[:, 0] * live_op[:, None, None]
    masked_pro = pro_tiles * pro_live.astype(jnp.float32)[:, :, None, None]
    op_where = jnp.stack([op_rows[:, 0], op_cols[:, 0] + col_index * fine_cols], axis=1)
    panel_tiles, panel_ids = column_panel(masked_pro, pro_cols)
    empty_product = jnp.zeros((fine_rows, coarse_cols, tile_size, tile_size), jnp.float32)
    piece_tiles = lax.all_gather(masked_op, "col", axis=0, tiled=True)
    piece_where = lax.all_gather(op_where, "col", axis=0, tiled=True)
    fine_ids = piece_where[:, 1]
    right_tiles = panel_tiles[fine_ids, 0]
    targets = panel_ids[fine_ids, 0]
    tile_prods = jnp.einsum("nab,nbc->nac", piece_tiles, right_tiles, precision=precise)
    product = empty_product.at[piece_where[:, 0], targets].add(tile_prods)
    panel_tiles, panel_ids = column_panel(masked_pro, pro_cols)
    root_col = row_index * coarse_rows // coarse_cols
    far_tiles, far_ids = (
        broadcast(panel_tiles, "col", root_col),
        broadcast(panel_ids, "col", root_col),
    )
    shift_ids = root_col * coarse_cols - row_index * coarse_rows
    empty_owned = jnp.zeros((coarse_rows, coarse_cols, tile_size, tile_size), jnp.float32)
    left_tiles = far_tiles
    left_ids = far_ids + shift_ids
    inside = (left_ids >= 0) & (left_ids < coarse_rows)
    left_tiles = left_tiles * inside.astype(jnp.float32)[:, :, None, None]
    tile_prods = jnp.einsum(
        "ksba,kjbc->ksjac",
        left_tiles,
        lax.all_gather(product, "row", axis=0, tiled=True),
        precision=precise,
    )
    placed = jnp.clip(left_ids, 0, coarse_rows - 1)
    coarse = empty_owned.at[placed.reshape(-1)].add(
        tile_prods.reshape((-1,) + tile_prods.shape[2:])
    )
    return (product, coarse)


def solution(mesh):
    return jax.shard_map(
        shards,
        mesh=mesh,
        in_specs=(
            P("row", "col", None, None),
            P("row", "col"),
            P("row", "col"),
            P("row", "col"),
            P("row", "col", None, None),
            P("row", "col"),
            P("row", "col"),
        ),
        out_specs=(P("row", "col", None, None), P("row", "col", None, None)),
        check_vma=False,
    )
```

profile of v0, /device:TPU:1, one launch (start us, length us, event | category | flops | bytes accessed | tf_op | source)
XLA Modules:
  0.0 547.0 jit_solution(2243945836866424324)
XLA Ops:
  7.2 0.0 copy-start.2
  7.2 0.0 all-gather.7.cloned.1.call-start
  7.2 0.7 convert_bitcast_fusion
  7.9 1.7 broadcast_multiply_fusion
  9.6 0.0 all-gather.7.cloned.1.call-update
  9.6 0.0 all-gather.5.cloned.1.call-start
  10.3 2.3 bitcast_multiply_fusion
  12.7 0.0 all-gather.5.cloned.1.call-update
  12.7 0.0 all-reduce.4.cloned.1.call-start
  12.8 0.7 broadcast_add_fusion
  13.4 0.7 add_bitcast_fusion
  14.1 30.4 %all-gather = s32[16,32,2]{1,2,0:T(2,128)S(1)} all-gather(s32[1,32,2]{1,2,0:T(2,128)S(1)} %add_bitcast_fusion), channel_id=1, replica_groups=mesh['row'=16,'col'=16] {'col'}, dimensions={0}, use_global_device_ids=true | all-gather | bytes 4352 | tf_op jit(solution)/shard_map/all_gather | solution.py:42
  44.5 0.1 reshape.70
  44.6 1.3 dynamic-slice
  46.5 30.3 %all-gather.7.cloned.1.call-done = f32[128,1,64,64]{3,2,1,0:T(8,128)} async-done(((f32[8,1,64,64]{3,2,1,0:T(8,128)}), f32[128,1,64,64]{3,2,1,0:T(8,128)}) %all-gather.7.cloned.1.call-update) | async-done | bytes 2097168 | tf_op jit(solution)/shard_map/all_gather | solution.py:17
  76.8 2.8 broadcast_select_fusion
  79.6 0.0 all-reduce.4.cloned.1.call-update
  79.6 0.0 all-gather.9.cloned.1.call-start
  79.7 0.0 copy-done.2
  79.7 0.1 bitcast_dynamic-update-slice_fusion
  79.8 8.3 %all-reduce.1 = s32[128]{0:T(128)S(1)} all-reduce(s32[128]{0:T(128)S(1)} %bitcast_dynamic-update-slice_fusion), channel_id=1, replica_groups=mesh['row'=16,'col'=16] {'row'}, use_global_device_ids=true, to_apply=%add.1 | all-reduce | flops 128 | bytes 1024
  88.1 3.5 gather_fusion
  91.7 11.7 %gather_fusion.1 = f32[512,64,64]{2,1,0:T(8,128)} fusion(f32[128,1,64,64]{3,2,1,0:T(8,128)} %all-gather.7.cloned.1.call-done, s32[512]{0:T(512)S(1)} %bitcast.41), kind=kCustom, calls=%fused_computation.1 | custom fusion | bytes 16781312 | tf_op jit(solution)/shard_map/gather | solution.py:44
  103.3 158.7 %all-gather.5.cloned.1.call-done = f32[512,64,64]{2,1,0:T(8,128)} async-done(((f32[32,64,64]{2,1,0:T(8,128)}), f32[512,64,64]{2,1,0:T(8,128)}) %all-gather.5.cloned.1.call-update) | async-done | bytes 8388624 | tf_op jit(solution)/shard_map/all_gather | solution.py:41
  262.1 23.9 %fusion.12 = f32[512,64,64]{2,1,0:T(8,128)} fusion(f32[512,64,64]{2,1,0:T(8,128)} %all-gather.5.cloned.1.call-done, f32[512,64,64]{2,1,0:T(8,128)} %gather_fusion.1), kind=kOutput, calls=%fused_computation.31 | convolution fusion | flops 1610612736 | bytes 25165824 | tf_op jit(solution)/shard_map/nab,nbc->nac/dot_general | solution.py:46
  286.0 55.8 %scatter_fusion = f32[8,2,64,64]{3,2,1,0:T(8,128)S(1)} fusion(f32[8,2,64,64]{3,2,1,0:T(8,128)S(1)} %broadcast_in_dim.6, s32[512]{0:T(512)S(1)} %bitcast.42, f32[512,64,64]{2,1,0:T(8,128)} %fusion.12), kind=kCustom, calls=%fused_computation.2 | custom fusion | flops 2097152 | bytes 25169920 | tf_op jit(solution)/shard_map/scatter-add | solution.py:47
  341.8 0.0 copy-start
  341.8 0.8 copy-done
  342.6 0.0 all-gather.9.cloned.1.call-update
  342.6 10.7 %psum.14 = s32[128,1]{0,1:T(1,128)S(1)} all-reduce(s32[128,1]{0,1:T(1,128)S(1)} %broadcast_select_fusion.1), channel_id=1, replica_groups=mesh['row'=16,'col'=16] {'col'}, use_global_device_ids=true, to_apply=%region_1.2 | all-reduce | flops 128 | bytes 1024 | tf_op jit(solution)/shard_map/psum | solution.py:12
  353.3 54.1 %all-reduce.4.cloned.1.call-done = f32[128,1,64,64]{3,2,1,0:T(8,128)} async-done(((f32[128,1,64,64]{3,2,1,0:T(8,128)}), f32[128,1,64,64]{3,2,1,0:T(8,128)}) %all-reduce.4.cloned.1.call-update) | async-done | bytes 2097168 | tf_op jit(solution)/shard_map/psum | solution.py:12
  407.4 87.7 %all-gather.9.cloned.1.call-done = f32[128,2,64,64]{3,2,1,0:T(8,128)} async-done(((f32[8,2,64,64]{3,2,1,0:T(8,128)}), f32[128,2,64,64]{3,2,1,0:T(8,128)}) %all-gather.9.cloned.1.call-update) | async-done | bytes 4194320 | tf_op jit(solution)/shard_map/all_gather | solution.py:63
  495.1 18.5 %fusion.3 = f32[128,2,64,64]{2,3,1,0:T(8,128)} fusion(f32[128,2,64,64]{3,2,1,0:T(8,128)} %all-gather.9.cloned.1.call-done, f32[128,1,64,64]{3,2,1,0:T(8,128)} %all-reduce.4.cloned.1.call-done, f32[128]{0:T(128)S(1)} %fusion.10), kind=kOutput, calls=%fused_computation.7 | convolution fusion | flops 805830656 | bytes 10486272 | tf_op jit(solution)/shard_map/ksba,kjbc->ksjac/dot_general | solution.py:60
  513.6 9.1 %copy.15 = f32[128,2,64,64]{3,2,1,0:T(8,128)} copy(f32[128,2,64,64]{2,3,1,0:T(8,128)} %fusion.3) | data formatting | bytes 8388608 | tf_op jit(solution)/shard_map/reshape | solution.py:68
  522.8 17.0 %scatter_fusion.1 = f32[2,2,64,64]{3,2,1,0:T(8,128)S(1)} fusion(f32[2,2,64,64]{3,2,1,0:T(8,128)S(1)} %broadcast_in_dim.7, s32[128]{0:T(128)S(1)} %fusion.11, f32[128,2,64,64]{3,2,1,0:T(8,128)} %copy.15), kind=kCustom, calls=%fused_computation.3 | custom fusion | flops 1048576 | bytes 12583424 | tf_op jit(solution)/shard_map/scatter-add | solution.py:67
  539.8 0.0 copy-start.1
  539.8 0.6 copy-done.1
  (10 shorter events, 0.1 us)
Async XLA Ops:
  7.2 72.5 %copy-start.2 = (s32[8,1]{0,1:T(1,128)S(1)}, s32[8,1]{0,1:T(1,128)}, u32[]{:S(2)}) copy-start(s32[8,1]{0,1:T(1,128)} %param.12) | copy-start | bytes 100
  7.2 69.6 %all-gather.7.cloned.1.call-start = ((), (), s32[]{:S(2)}) async-start(), calls=%async_computation.1 | async-start | bytes 4456448 | tf_op jit(solution)/shard_map/all_gather | solution.py:17
  9.6 252.4 %all-gather.5.cloned.1.call-start = ((), (), s32[]{:S(2)}) async-start(), calls=%async_computation | async-start | bytes 17825792 | tf_op jit(solution)/shard_map/all_gather | solution.py:41
  12.7 394.7 %all-reduce.4.cloned.1.call-start = ((), (), s32[]{:S(2)}) async-start(), calls=%async_computation.3 | async-start | bytes 8388608 | tf_op jit(solution)/shard_map/psum | solution.py:12
  79.6 415.5 %all-gather.9.cloned.1.call-start = ((), (), s32[]{:S(2)}) async-start(), calls=%async_computation.2 | async-start | bytes 8912896 | tf_op jit(solution)/shard_map/all_gather | solution.py:63
  341.8 0.8 copy-start
  539.8 0.7 copy-start.1
Sparse Core Ops, SparseCore 0:
  11.3 65.4 all-gather.6
  78.6 183.4 all-gather.4
  264.8 142.5 all-reduce.3
  410.5 84.5 all-gather.8
where the time goes:
time: 549 us; the launch traced here: 547 us
  waiting for transfers between devices  331 us (60%)
  other arithmetic  81.6 us (15%)
  blocking collectives  49.4 us (9%)
  matrix products  42.4 us (8%)
  local copies, waits for them, and re-layouts  27.2 us (5%)
  between operations  15.2 us (3%)
    all_gather x1, waiting for transfers between devices, shards(): piece_tiles = lax.all_gather(masked_op, 'col', axis=0, tiled=True)  159 us
    all_gather x1, waiting for transfers between devices, shards(): lax.all_gather(product, 'row', axis=0, tiled=True)  87.7 us
    scatter-add x1, other arithmetic, shards(): product = empty_product.at[piece_where[:, 0], targets].add(tile_prods)  55.8 us
    psum x1, waiting for transfers between devices, broadcast(): return lax.psum(jnp.where(mine, value, jnp.zeros_like(value)), axis)  54.1 us
    all_gather x1, blocking collectives, shards(): piece_where = lax.all_gather(op_where, 'col', axis=0, tiled=True)  30.4 us
    all_gather x1, waiting for transfers between devices, column_panel(): lax.all_gather(masked_pro, 'row', axis=0, tiled=True)  30.3 us
    dot_general x1, matrix products, shards(): jnp.einsum('nab,nbc->nac', piece_tiles, right_tiles, precision=precise)  23.9 us
    dot_general x1, matrix products, shards(): jnp.einsum('ksba,kjbc->ksjac', left_tiles, lax.all_gather(product, 'row',...  18.5 us
  transfers between devices with their start and end apart: 4, of which 4 were waited for; matrix products, arithmetic and copies ran while one was open for 19% of the time, Pallas kernels for 0%

commit v1 on v0

--- a/solution.py
+++ b/solution.py
@@ -1,3 +1,4 @@
+import functools
 import jax
 import jax.numpy as jnp
 from jax import lax
@@ -5,6 +6,18 @@
 
 COARSEN = 4
 precise = lax.Precision.HIGHEST
+
+
+def lots_all_advance(obj, which_axis):
+    return jnp.concatenate(
+        lax.all_to_all(
+            jnp.stack([obj for _ in range(lax.psum(1, which_axis))], 0), which_axis, 0, 0
+        ),
+        axis=0,
+    )
+
+
+report_digits_now = functools.partial(lots_all_advance, which_axis="row")
 
 
 def broadcast(value, axis, root):
@@ -58,10 +71,7 @@
     inside = (left_ids >= 0) & (left_ids < coarse_rows)
     left_tiles = left_tiles * inside.astype(jnp.float32)[:, :, None, None]
     tile_prods = jnp.einsum(
-        "ksba,kjbc->ksjac",
-        left_tiles,
-        lax.all_gather(product, "row", axis=0, tiled=True),
-        precision=precise,
+        "ksba,kjbc->ksjac", left_tiles, report_digits_now(product), precision=precise
     )
     placed = jnp.clip(left_ids, 0, coarse_rows - 1)
     coarse = empty_owned.at[placed.reshape(-1)].add(

time: 549 us -> 587 us (1.069)
  the two profiles are of different devices: /device:TPU:1 before, /device:TPU:2 now
where the time goes in v1:
time: 587 us; the launch traced here: 585 us
  waiting for transfers between devices  247 us (42%)
  blocking collectives  131 us (22%)
  other arithmetic  95.2 us (16%)
  local copies, waits for them, and re-layouts  52.1 us (9%)
  matrix products  36.5 us (6%)
  between operations  15.2 us (3%)
  starting transfers between devices  7.1 us (1%)
    all_gather x1, waiting for transfers between devices, shards(): piece_tiles = lax.all_gather(masked_op, 'col', axis=0, tiled=True)  174 us
    psum x1, blocking collectives, broadcast(): return lax.psum(jnp.where(mine, value, jnp.zeros_like(value)), axis)  82.1 us
    psum x1, waiting for transfers between devices, broadcast(): return lax.psum(jnp.where(mine, value, jnp.zeros_like(value)), axis)  65.4 us
    scatter-add x1, other arithmetic, shards(): product = empty_product.at[piece_where[:, 0], targets].add(tile_prods)  55.6 us
    all_gather x1, blocking collectives, shards(): piece_where = lax.all_gather(op_where, 'col', axis=0, tiled=True)  36.4 us
    unnamed x11, local copies, waits for them, and re-layouts  27.2 us
    dot_general x1, matrix products, shards(): jnp.einsum('nab,nbc->nac', piece_tiles, right_tiles, precision=precise)  23.8 us
    scatter-add x1, other arithmetic, shards(): empty_owned.at[placed.reshape(-1)]  17 us
  transfers between devices with their start and end apart: 4, of which 4 were waited for; matrix products, arithmetic and copies ran while one was open for 8% of the time, Pallas kernels for 0%

profile of v1, /device:TPU:2, one launch (start us, length us, event | category | flops | bytes accessed | tf_op | source)
XLA Modules:
  0.0 584.7 jit_solution(10219009736339331927)
XLA Ops:
  7.2 0.0 all-gather.6.cloned.1.call-start
  7.2 0.7 convert_bitcast_fusion
  7.9 1.7 broadcast_multiply_fusion
  9.6 0.0 all-gather.6.cloned.1.call-update
  9.6 0.0 all-gather.4.cloned.1.call-start
  10.3 2.3 bitcast_multiply_fusion
  12.7 0.0 all-gather.4.cloned.1.call-update
  12.7 0.7 broadcast_add_fusion
  13.4 0.7 add_bitcast_fusion
  14.0 36.4 %all-gather = s32[16,32,2]{1,2,0:T(2,128)S(1)} all-gather(s32[1,32,2]{1,2,0:T(2,128)S(1)} %add_bitcast_fusion), channel_id=1, replica_groups=mesh['row'=16,'col'=16] {'col'}, dimensions={0}, use_global_device_ids=true | all-gather | bytes 4352 | tf_op jit(solution)/shard_map/all_gather | solution.py:55
  50.5 0.1 reshape.76
  50.6 1.3 dynamic-slice
  52.5 0.8 bitcast_dynamic-update-slice_fusion
  53.3 12.6 %all-reduce.1 = s32[128]{0:T(128)S(1)} all-reduce(s32[128]{0:T(128)S(1)} %bitcast_dynamic-update-slice_fusion), channel_id=1, replica_groups=mesh['row'=16,'col'=16] {'row'}, use_global_device_ids=true, to_apply=%add.1 | all-reduce | flops 128 | bytes 1024
  65.8 3.5 gather_fusion
  69.4 6.0 %all-gather.6.cloned.1.call-done = f32[128,1,64,64]{3,2,1,0:T(8,128)} async-done(((f32[8,1,64,64]{3,2,1,0:T(8,128)}), f32[128,1,64,64]{3,2,1,0:T(8,128)}) %all-gather.6.cloned.1.call-update) | async-done | bytes 2097168 | tf_op jit(solution)/shard_map/all_gather | solution.py:30
  75.4 11.7 %gather_fusion.1 = f32[512,64,64]{2,1,0:T(8,128)} fusion(f32[128,1,64,64]{3,2,1,0:T(8,128)} %all-gather.6.cloned.1.call-done, s32[512]{0:T(512)S(1)} %bitcast.45), kind=kCustom, calls=%fused_computation.1 | custom fusion | bytes 16781312 | tf_op jit(solution)/shard_map/gather | solution.py:57
  87.0 174.5 %all-gather.4.cloned.1.call-done = f32[512,64,64]{2,1,0:T(8,128)} async-done(((f32[32,64,64]{2,1,0:T(8,128)}), f32[512,64,64]{2,1,0:T(8,128)}) %all-gather.4.cloned.1.call-update) | async-done | bytes 8388624 | tf_op jit(solution)/shard_map/all_gather | solution.py:54
  261.5 23.8 %fusion.12 = f32[512,64,64]{2,1,0:T(8,128)} fusion(f32[512,64,64]{2,1,0:T(8,128)} %all-gather.4.cloned.1.call-done, f32[512,64,64]{2,1,0:T(8,128)} %gather_fusion.1), kind=kOutput, calls=%fused_computation.32 | convolution fusion | flops 1610612736 | bytes 25165824 | tf_op jit(solution)/shard_map/nab,nbc->nac/dot_general | solution.py:59
  285.3 55.6 %scatter_fusion = f32[8,2,64,64]{3,2,1,0:T(8,128)S(1)} fusion(f32[8,2,64,64]{3,2,1,0:T(8,128)S(1)} %broadcast_in_dim.6, s32[512]{0:T(512)S(1)} %bitcast.46, f32[512,64,64]{2,1,0:T(8,128)} %fusion.12), kind=kCustom, calls=%fused_computation.2 | custom fusion | flops 2097152 | bytes 25169920 | tf_op jit(solution)/shard_map/scatter-add | solution.py:60
  340.9 0.0 copy-start
  340.9 0.2 copy.14
  341.1 4.3 broadcast_bitcast_fusion
  345.4 13.3 %reshape.80 = f32[16,1,65536]{2,1,0:T(1,128)} reshape(f32[16,8,2,64,64]{4,3,2,1,0:T(8,128)} %broadcast_bitcast_fusion) | data formatting | bytes 8388608
  358.7 0.0 copy-done
  358.7 7.0 %all-to-all-start = ((f32[16,1,65536]{2,1,0:T(1,128)}), f32[16,1,65536]{2,1,0:T(1,128)}, u32[]{:S(2)}, u32[]{:S(2)}) async-start(f32[16,1,65536]{2,1,0:T(1,128)} %reshape.80), calls=%async_computation | async-start | bytes 8388608 | tf_op jit(solution)/shard_map/all_to_all | solution.py:13
  365.7 0.0 all-reduce.4.cloned.1.call-start
  365.7 2.8 broadcast_select_fusion
  368.5 0.0 all-reduce.4.cloned.1.call-update
  368.6 82.1 %psum.14 = s32[128,1]{0,1:T(1,128)S(1)} all-reduce(s32[128,1]{0,1:T(1,128)S(1)} %broadcast_select_fusion.1), channel_id=1, replica_groups=mesh['row'=16,'col'=16] {'col'}, use_global_device_ids=true, to_apply=%region_1.2 | all-reduce | flops 128 | bytes 1024 | tf_op jit(solution)/shard_map/psum | solution.py:25
  450.8 1.4 all-to-all-done
  452.2 0.5 broadcast.109
  452.7 13.7 %reduce = f32[16,65536]{1,0:T(8,128)} reduce(f32[16,1,65536]{2,1,0:T(1,128)} %all-to-all-done, f32[]{:T(128)} %broadcast.109), dimensions={1}, to_apply=%all_to_all.3.reduce_sub_computation | reduce | bytes 8388612 | tf_op jit(solution)/shard_map/all_to_all | solution.py:13
  466.4 6.9 %reshape.81 = f32[16,8,2,64,64]{4,3,2,1,0:T(8,128)} reshape(f32[16,65536]{1,0:T(8,128)} %reduce) | data formatting | bytes 8388608
  473.3 65.4 %all-reduce.4.cloned.1.call-done = f32[128,1,64,64]{3,2,1,0:T(8,128)} async-done(((f32[128,1,64,64]{3,2,1,0:T(8,128)}), f32[128,1,64,64]{3,2,1,0:T(8,128)}) %all-reduce.4.cloned.1.call-update) | async-done | bytes 2097168 | tf_op jit(solution)/shard_map/psum | solution.py:25
  538.7 12.8 %fusion.3 = f32[128,2,64,64]{2,3,1,0:T(8,128)} fusion(f32[128,2,64,64]{2,3,1,0:T(8,128)} %bitcast.47, f32[128,1,64,64]{3,2,1,0:T(8,128)} %all-reduce.4.cloned.1.call-done, f32[128]{0:T(128)S(1)} %fusion.10), kind=kOutput, calls=%fused_computation.7 | convolution fusion | flops 805830656 | bytes 10486272 | tf_op jit(solution)/shard_map/ksba,kjbc->ksjac/dot_general | solution.py:73
  551.5 9.0 %copy.15 = f32[128,2,64,64]{3,2,1,0:T(8,128)} copy(f32[128,2,64,64]{2,3,1,0:T(8,128)} %fusion.3) | data formatting | bytes 8388608 | tf_op jit(solution)/shard_map/reshape | solution.py:78
  560.5 17.0 %scatter_fusion.1 = f32[2,2,64,64]{3,2,1,0:T(8,128)S(1)} fusion(f32[2,2,64,64]{3,2,1,0:T(8,128)S(1)} %broadcast_in_dim.7, s32[128]{0:T(128)S(1)} %fusion.11, f32[128,2,64,64]{3,2,1,0:T(8,128)} %copy.15), kind=kCustom, calls=%fused_computation.3 | custom fusion | flops 1048576 | bytes 12583424 | tf_op jit(solution)/shard_map/scatter-add | solution.py:77
  577.5 0.0 copy-start.1
  577.5 0.6 copy-done.1
  (10 shorter events, 0.1 us)
Async XLA Ops:
  7.2 68.2 %all-gather.6.cloned.1.call-start = ((), (), s32[]{:S(2)}) async-start(), calls=%async_computation.2 | async-start | bytes 4456448 | tf_op jit(solution)/shard_map/all_gather | solution.py:30
  9.6 251.9 %all-gather.4.cloned.1.call-start = ((), (), s32[]{:S(2)}) async-start(), calls=%async_computation.1 | async-start | bytes 17825792 | tf_op jit(solution)/shard_map/all_gather | solution.py:54
  340.9 17.8 %copy-start = (f32[8,2,64,64]{3,2,1,0:T(8,128)}, f32[8,2,64,64]{3,2,1,0:T(8,128)S(1)}, u32[]{:S(2)}) copy-start(f32[8,2,64,64]{3,2,1,0:T(8,128)S(1)} %scatter_fusion) | copy-start | bytes 786436
  358.7 93.5 %all-to-all-start = ((f32[16,1,65536]{2,1,0:T(1,128)}), f32[16,1,65536]{2,1,0:T(1,128)}, u32[]{:S(2)}, u32[]{:S(2)}) async-start(f32[16,1,65536]{2,1,0:T(1,128)} %reshape.80), calls=%async_computation | async-start | bytes 8388608 | tf_op jit(solution)/shard_map/all_to_all | solution.py:13
  365.7 173.0 %all-reduce.4.cloned.1.call-start = ((), (), s32[]{:S(2)}) async-start(), calls=%async_computation.3 | async-start | bytes 8388608 | tf_op jit(solution)/shard_map/psum | solution.py:25
  577.5 0.7 copy-start.1
Sparse Core Ops, SparseCore 0:
  11.3 64.0 all-gather.5
  77.1 184.3 all-gather.3
  369.1 169.5 all-reduce.3
